TPU v7x, 512 devices: a whole 4x8x8 slice. The times are simulated.
512 devices in a mesh: row: 32 (over x, y), col: 8 (over z_hi, core), vec: 2 (over z_lo).
Axes of the slice: x: 4, y: 8, z: 8 (z_hi: 4, z_lo: 2; z = z_hi * 2 + z_lo), core: 2. Of those that a mesh axis runs over, the one named last changes fastest.
Arguments:
- vectors: bfloat16 [131072, 256], P(('row', 'col'), 'vec'), parts along dimension 1, may hold values from -6 to 6
- tile_blocks: bfloat16 [32, 8, 32, 256, 256], P('row', 'col'), may hold values from -0.125 to 0.125
- block_rows: int32 [32, 8, 32], P('row', 'col'), may hold values from 0 to 15, as said below
- block_cols: int32 [32, 8, 32], P('row', 'col'), may hold values from 0 to 63, as said below
- counts: int32 [32, 8], P('row', 'col'), may hold values from 1 to 32, as said below
Outputs:
- filtered: bfloat16 [131072, 256], P(('row', 'col'), 'vec'), parts along dimension 1
There are 2 independent parts, one for each index of `vec`. A program takes and returns all parts, laid end to end along the dimension named above; an argument that names none is the same for every part. Nothing has to cross between parts.
Inputs may be any that keep to these rules, and one draw needn't show every extreme that they name: The pairs (block_rows, block_cols // 2) of the 32 slots of one tile are all distinct. Within one tile, all slots whose block columns lie in the same group of 2 (same block_cols // 2) name the same block column. `counts`: some tile uses all 32 slots.
All inputs are finite; a program needn't handle non-finite values.
Results may differ from a plain program's by a relative error of at most 0.015.
Values may be sent and summed in bfloat16 or wider, within the bound.
A program may use at most 64 MiB of HBM per device.

v0:
```python
import jax
import jax.numpy as jnp
from jax import lax
from jax.sharding import PartitionSpec as P

DEGREE = 3
center_value = 0.5
half_width = 2.0


def on_device(vectors, tile_blocks, block_rows, block_cols, counts):
    n_row = lax.axis_size("row")
    n_col = lax.axis_size("col")
    tile_data = tile_blocks[0, 0]
    slot_rows = block_rows[0, 0]
    slot_cols = block_cols[0, 0]
    used = counts[0, 0]
    block_size = tile_data.shape[-1]
    width = vectors.shape[1]
    piece_blocks = vectors.shape[0] // block_size
    row_blocks = piece_blocks * n_col
    slot_count = tile_data.shape[0]
    live = (jnp.arange(slot_count) < used).astype(jnp.float32)
    onehot = (slot_rows[None, :] == jnp.arange(row_blocks)[:, None]).astype(jnp.float32) * live[
        None, :
    ]

    def apply_tiles(current):
        gathered = lax.all_gather(current, "row", axis=0, tiled=True)
        vec_blocks = jnp.take(
            gathered.reshape(n_row * piece_blocks, block_size, width), slot_cols, axis=0
        )
        products = jnp.einsum(
            "sij,sjk->sik", tile_data, vec_blocks, preferred_element_type=jnp.float32
        )
        term = jnp.einsum("ls,sik->lik", onehot, products, precision=lax.Precision.HIGHEST)
        term = term.reshape(row_blocks * block_size, width)
        return lax.psum_scatter(
            term.astype(jnp.bfloat16), "col", scatter_dimension=0, tiled=True
        ).astype(jnp.float32)

    previous = vectors
    applied = apply_tiles(vectors)
    current = ((applied - center_value * previous.astype(jnp.float32)) / half_width).astype(
        jnp.bfloat16
    )
    for repeat in range(DEGREE - 1):
        applied = apply_tiles(current)
        following = (
            2.0 * (applied - center_value * current.astype(jnp.float32)) / half_width
            - previous.astype(jnp.float32)
        ).astype(jnp.bfloat16)
        previous, current = (current, following)
    return current


def solution(mesh):
    return jax.shard_map(
        on_device,
        mesh=mesh,
        in_specs=(
            P(("row", "col"), "vec"),
            P("row", "col", None, None, None),
            P("row", "col", None),
            P("row", "col", None),
            P("row", "col"),
        ),
        out_specs=P(("row", "col"), "vec"),
        check_vma=False,
    )
```

profile of v0, /device:TPU:2, one launch (start us, length us, event | category | flops | bytes accessed | tf_op | source)
XLA Modules:
  0.0 470.1 jit_solution(5632547068831693479)
XLA Ops:
  6.5 0.0 all-gather.4.cloned.1.call-start
  6.5 0.7 all-gather.4.cloned.1.call-update
  7.3 0.0 reduce-scatter.4.cloned.1.call-start
  8.0 0.7 compare_select_fusion
  8.6 0.7 compare_and_fusion
  9.3 91.6 %all-gather.4.cloned.1.call-done = bf16[16384,128]{1,0:T(8,128)(2,1)} async-done(((bf16[512,128]{1,0:T(8,128)(2,1)}), bf16[16384,128]{1,0:T(8,128)(2,1)}) %all-gather.4.cloned.1.call-update) | async-done | bytes 4194320 | tf_op jit(solution)/shard_map/all_gather | solution.py:29
  100.9 3.1 gather_fusion
  104.1 6.6 %fusion.10 = f32[32,128,256]{2,1,0:T(8,128)} fusion(bf16[1,1,32,256,256]{4,3,2,1,0:T(8,128)(2,1)} %param.8, bf16[32,256,128]{2,1,0:T(8,128)(2,1)S(1)} %gather_fusion, pred[32]{0:T(512)(128)(4,1)S(1)} %compare_and_fusion), kind=kOutput, calls=%fused_computation.13 | convolution fusion | flops 537919488 | bytes 10485792 | tf_op jit(solution)/shard_map/sij,sjk->sik/dot_general | solution.py:33
  110.6 0.0 copy-start.3
  110.6 5.5 %copy.9 = f32[32,128,256]{1,0,2:T(8,128)} copy(f32[32,128,256]{2,1,0:T(8,128)} %fusion.10) | data formatting | bytes 8388608 | tf_op jit(solution)/shard_map/sij,sjk->sik/dot_general | solution.py:33
  116.2 0.0 copy-done.3
  116.2 0.0 copy-start.1
  116.2 4.3 fusion.18
  120.5 1.2 copy.6
  121.7 0.0 reduce-scatter.4.cloned.1.call-update
  121.8 0.0 all-gather.6.cloned.1.call-start
  121.8 41.6 %reduce-scatter.4.cloned.1.call-done = bf16[512,128]{1,0:T(8,128)(2,1)} async-done(((bf16[4096,128]{1,0:T(8,128)(2,1)}), bf16[512,128]{1,0:T(8,128)(2,1)}) %reduce-scatter.4.cloned.1.call-update) | async-done | bytes 131088 | tf_op jit(solution)/shard_map/reduce_scatter | solution.py:38
  163.4 0.0 copy-done.1
  163.4 1.6 fusion.32
  165.0 0.0 all-gather.6.cloned.1.call-update
  165.1 0.0 reduce-scatter.6.cloned.1.call-start
  165.1 84.9 %all-gather.6.cloned.1.call-done = bf16[16384,128]{1,0:T(8,128)(2,1)} async-done(((bf16[512,128]{1,0:T(8,128)(2,1)}), bf16[16384,128]{1,0:T(8,128)(2,1)}) %all-gather.6.cloned.1.call-update) | async-done | bytes 4194320 | tf_op jit(solution)/shard_map/all_gather | solution.py:29
  250.0 3.1 gather_fusion.1
  253.1 6.6 %fusion.8 = f32[32,128,256]{2,1,0:T(8,128)} fusion(bf16[1,1,32,256,256]{4,3,2,1,0:T(8,128)(2,1)} %param.8, bf16[32,256,128]{2,1,0:T(8,128)(2,1)S(1)} %gather_fusion.1, pred[32]{0:T(512)(128)(4,1)S(1)} %compare_and_fusion), kind=kOutput, calls=%fused_computation.11 | convolution fusion | flops 537919488 | bytes 10485792 | tf_op jit(solution)/shard_map/sij,sjk->sik/dot_general | solution.py:33
  259.7 5.5 %copy.10 = f32[32,128,256]{1,0,2:T(8,128)} copy(f32[32,128,256]{2,1,0:T(8,128)} %fusion.8) | data formatting | bytes 8388608 | tf_op jit(solution)/shard_map/sij,sjk->sik/dot_general | solution.py:33
  265.2 0.0 copy-start
  265.2 4.3 fusion.21
  269.5 1.2 copy.7
  270.8 0.0 reduce-scatter.6.cloned.1.call-update
  270.8 0.0 all-gather.8.cloned.1.call-start
  270.9 41.7 %reduce-scatter.6.cloned.1.call-done = bf16[512,128]{1,0:T(8,128)(2,1)} async-done(((bf16[4096,128]{1,0:T(8,128)(2,1)}), bf16[512,128]{1,0:T(8,128)(2,1)}) %reduce-scatter.6.cloned.1.call-update) | async-done | bytes 131088 | tf_op jit(solution)/shard_map/reduce_scatter | solution.py:38
  312.5 0.0 copy-done
  312.6 1.6 fusion.33
  314.2 0.0 all-gather.8.cloned.1.call-update
  314.2 0.2 reduce-scatter.8.cloned.1.call-start
  314.4 84.6 %all-gather.8.cloned.1.call-done = bf16[16384,128]{1,0:T(8,128)(2,1)} async-done(((bf16[512,128]{1,0:T(8,128)(2,1)}), bf16[16384,128]{1,0:T(8,128)(2,1)}) %all-gather.8.cloned.1.call-update) | async-done | bytes 4194320 | tf_op jit(solution)/shard_map/all_gather | solution.py:29
  399.0 3.1 gather_fusion.2
  402.2 6.6 %fusion.6 = f32[32,128,256]{2,1,0:T(8,128)} fusion(bf16[1,1,32,256,256]{4,3,2,1,0:T(8,128)(2,1)} %param.8, bf16[32,256,128]{2,1,0:T(8,128)(2,1)S(1)} %gather_fusion.2, pred[32]{0:T(512)(128)(4,1)S(1)} %compare_and_fusion), kind=kOutput, calls=%fused_computation.9 | convolution fusion | flops 537919488 | bytes 10485792 | tf_op jit(solution)/shard_map/sij,sjk->sik/dot_general | solution.py:33
  408.8 5.5 %copy.11 = f32[32,128,256]{1,0,2:T(8,128)} copy(f32[32,128,256]{2,1,0:T(8,128)} %fusion.6) | data formatting | bytes 8388608 | tf_op jit(solution)/shard_map/sij,sjk->sik/dot_general | solution.py:33
  414.3 0.0 copy-start.2
  414.3 4.3 fusion.24
  418.6 1.2 copy.8
  419.8 0.0 reduce-scatter.8.cloned.1.call-update
  419.9 41.7 %reduce-scatter.8.cloned.1.call-done = bf16[512,128]{1,0:T(8,128)(2,1)} async-done(((bf16[4096,128]{1,0:T(8,128)(2,1)}), bf16[512,128]{1,0:T(8,128)(2,1)}) %reduce-scatter.8.cloned.1.call-update) | async-done | bytes 131088 | tf_op jit(solution)/shard_map/reduce_scatter | solution.py:38
  461.6 0.0 copy-done.2
  461.6 1.6 fusion.35
  (2 shorter events, 0.0 us)
Async XLA Ops:
  6.5 94.4 %all-gather.4.cloned.1.call-start = ((), (), s32[]{:S(2)}) async-start(), calls=%async_computation.3 | async-start | bytes 4325376 | tf_op jit(solution)/shard_map/all_gather | solution.py:29
  7.3 156.2 %reduce-scatter.4.cloned.1.call-start = ((), (), s32[]{:S(2)}) async-start(), calls=%async_computation.4 | async-start | bytes 1179648 | tf_op jit(solution)/shard_map/reduce_scatter | solution.py:38
  110.6 5.5 %copy-start.3 = (s32[1,1,32]{2,1,0:T(1,128)S(1)}, s32[1,1,32]{2,1,0:T(1,128)}, u32[]{:S(2)}) copy-start(s32[1,1,32]{2,1,0:T(1,128)} %param.9) | copy-start | bytes 388
  116.2 47.2 %copy-start.1 = (bf16[512,128]{1,0:T(8,128)(2,1)S(1)}, bf16[512,128]{1,0:T(8,128)(2,1)}, u32[]{:S(2)}) copy-start(bf16[512,128]{1,0:T(8,128)(2,1)} %param.7) | copy-start | bytes 393220
  121.8 128.2 %all-gather.6.cloned.1.call-start = ((), (), s32[]{:S(2)}) async-start(), calls=%async_computation.5 | async-start | bytes 4325376 | tf_op jit(solution)/shard_map/all_gather | solution.py:29
  165.1 147.5 %reduce-scatter.6.cloned.1.call-start = ((), (), s32[]{:S(2)}) async-start(), calls=%async_computation.6 | async-start | bytes 1179648 | tf_op jit(solution)/shard_map/reduce_scatter | solution.py:38
  265.2 47.3 %copy-start = (bf16[512,128]{1,0:T(8,128)(2,1)S(1)}, bf16[512,128]{1,0:T(8,128)(2,1)}, u32[]{:S(2)}) copy-start(bf16[512,128]{1,0:T(8,128)(2,1)} %fusion.32) | copy-start | bytes 393220
  270.8 128.2 %all-gather.8.cloned.1.call-start = ((), (), s32[]{:S(2)}) async-start(), calls=%async_computation.7 | async-start | bytes 4325376 | tf_op jit(solution)/shard_map/all_gather | solution.py:29
  314.2 147.4 %reduce-scatter.8.cloned.1.call-start = ((), (), s32[]{:S(2)}) async-start(), calls=%async_computation.8 | async-start | bytes 1179648 | tf_op jit(solution)/shard_map/reduce_scatter | solution.py:38
  414.3 47.3 %copy-start.2 = (bf16[512,128]{1,0:T(8,128)(2,1)S(1)}, bf16[512,128]{1,0:T(8,128)(2,1)}, u32[]{:S(2)}) copy-start(bf16[512,128]{1,0:T(8,128)(2,1)} %fusion.33) | copy-start | bytes 393220
Sparse Core Ops, SparseCore 0:
  10.5 90.3 all-gather.3
  121.9 41.4 reduce-scatter.3
  166.6 83.3 all-gather.5
  270.9 41.5 reduce-scatter.5
  315.6 83.4 all-gather.7
  420.0 41.5 reduce-scatter.7
where the time goes:
time: 471 us; the launch traced here: 470 us
  waiting for transfers between devices  387 us (82%)
  matrix products  32.6 us (7%)
  local copies, waits for them, and re-layouts  29.7 us (6%)
  between operations  14.2 us (3%)
  other arithmetic  6.19 us (1%)
    all_gather x3, waiting for transfers between devices, apply_tiles(): gathered = lax.all_gather(current, 'row', axis=0, tiled=True)  261 us
    reduce_scatter x3, waiting for transfers between devices, apply_tiles(): lax.psum_scatter(term.astype(jnp.bfloat16), 'col', scatter_dimension=0, t...  125 us
    dot_general x3, matrix products, apply_tiles(): jnp.einsum('sij,sjk->sik', tile_data, vec_blocks, preferred_element_type=...  19.7 us
    dot_general x3, local copies, waits for them, and re-layouts, apply_tiles(): jnp.einsum('sij,sjk->sik', tile_data, vec_blocks, preferred_element_type=...  16.5 us
    dot_general x3, matrix products, apply_tiles(): jnp.einsum('ls,sik->lik', onehot, products, precision=lax.Precision.HIGHEST)  12.9 us
  transfers between devices with their start and end apart: 6, of which 6 were waited for; matrix products, arithmetic and copies ran while one was open for 0% of the time, Pallas kernels for 0%

commit v1 on v0

--- a/solution.py
+++ b/solution.py
@@ -26,7 +26,10 @@
     ]
 
     def apply_tiles(current):
-        gathered = lax.all_gather(current, "row", axis=0, tiled=True)
+        size = lax.axis_size("row")
+        tiles = jnp.stack([current for _ in range(size)])
+        tiles = lax.all_to_all(tiles, "row", split_axis=0, concat_axis=0)
+        gathered = jnp.concatenate(tiles, axis=0)
         vec_blocks = jnp.take(
             gathered.reshape(n_row * piece_blocks, block_size, width), slot_cols, axis=0
         )

time: 471 us -> 518 us (1.100)
  the two profiles are of different devices: /device:TPU:2 before, /device:TPU:4 now
where the time goes in v1:
time: 518 us; the launch traced here: 517 us
  waiting for transfers between devices  218 us (42%)
  blocking collectives  203 us (39%)
  local copies, waits for them, and re-layouts  35.3 us (7%)
  matrix products  32.5 us (6%)
  between operations  13.9 us (3%)
  starting transfers between devices  10.8 us (2%)
    all_to_all x2, blocking collectives, apply_tiles(): tiles = lax.all_to_all(tiles, 'row', split_axis=0, concat_axis=0)  203 us
    reduce_scatter x3, waiting for transfers between devices, apply_tiles(): lax.psum_scatter(term.astype(jnp.bfloat16), 'col', scatter_dimension=0, t...  124 us
    all_to_all x1, waiting for transfers between devices, apply_tiles(): tiles = lax.all_to_all(tiles, 'row', split_axis=0, concat_axis=0)  93.8 us
    dot_general x3, matrix products, apply_tiles(): jnp.einsum('sij,sjk->sik', tile_data, vec_blocks, preferred_element_type=...  19.7 us
    dot_general x3, local copies, waits for them, and re-layouts, apply_tiles(): jnp.einsum('sij,sjk->sik', tile_data, vec_blocks, preferred_element_type=...  16.5 us
    dot_general x3, matrix products, apply_tiles(): jnp.einsum('ls,sik->lik', onehot, products, precision=lax.Precision.HIGHEST)  12.9 us
    all_to_all x1, starting transfers between devices, apply_tiles(): tiles = lax.all_to_all(tiles, 'row', split_axis=0, concat_axis=0)  10.5 us
  transfers between devices with their start and end apart: 4, of which 4 were waited for; matrix products, arithmetic and copies ran while one was open for 0% of the time, Pallas kernels for 0%

profile of v1, /device:TPU:4, one launch (start us, length us, event | category | flops | bytes accessed | tf_op | source)
XLA Modules:
  0.0 517.5 jit_solution(16131196851127831485)
XLA Ops:
  6.5 3.8 stack.6
  10.4 0.0 copy-start.2
  10.4 10.5 %all-to-all-start = ((bf16[32,512,128]{2,1,0:T(8,128)(2,1)}), bf16[32,512,128]{2,1,0:T(8,128)(2,1)}, u32[]{:S(2)}, u32[]{:S(2)}) async-start(bf16[32,512,128]{2,1,0:T(8,128)(2,1)} %stack.6), calls=%async_computation | async-start | bytes 8388608 | tf_op jit(solution)/shard_map/all_to_all | solution.py:31
  20.9 0.0 reduce-scatter.4.cloned.1.call-start
  21.6 0.0 copy-done.2
  21.6 93.8 %all-to-all-done = bf16[32,512,128]{2,1,0:T(8,128)(2,1)} async-done(((bf16[32,512,128]{2,1,0:T(8,128)(2,1)}), bf16[32,512,128]{2,1,0:T(8,128)(2,1)}, u32[]{:S(2)}, u32[]{:S(2)}) %all-to-all-start) | async-done | bytes 4194336 | tf_op jit(solution)/shard_map/all_to_all | solution.py:31
  115.5 3.1 gather_fusion
  118.6 6.6 %fusion.10 = f32[32,128,256]{2,1,0:T(8,128)} fusion(bf16[1,1,32,256,256]{4,3,2,1,0:T(8,128)(2,1)} %param.8, bf16[32,256,128]{2,1,0:T(8,128)(2,1)S(1)} %gather_fusion, pred[32]{0:T(512)(128)(4,1)S(1)} %compare_and_fusion), kind=kOutput, calls=%fused_computation.13 | convolution fusion | flops 537919488 | bytes 10485792 | tf_op jit(solution)/shard_map/sij,sjk->sik/dot_general | solution.py:36
  125.2 0.0 copy-start.1
  125.2 5.5 %copy.9 = f32[32,128,256]{1,0,2:T(8,128)} copy(f32[32,128,256]{2,1,0:T(8,128)} %fusion.10) | data formatting | bytes 8388608 | tf_op jit(solution)/shard_map/sij,sjk->sik/dot_general | solution.py:36
  130.7 0.0 copy-done.1
  130.7 0.0 copy-start
  130.7 4.3 fusion.18
  135.0 1.2 copy.6
  136.3 0.0 reduce-scatter.4.cloned.1.call-update
  136.3 0.0 reduce-scatter.6.cloned.1.call-start
  136.3 45.0 %reduce-scatter.4.cloned.1.call-done = bf16[512,128]{1,0:T(8,128)(2,1)} async-done(((bf16[4096,128]{1,0:T(8,128)(2,1)}), bf16[512,128]{1,0:T(8,128)(2,1)}) %reduce-scatter.4.cloned.1.call-update) | async-done | bytes 131088 | tf_op jit(solution)/shard_map/reduce_scatter | solution.py:41
  181.3 0.0 copy-done
  181.3 1.0 fusion.32
  182.3 0.9 stack.7
  183.2 101.7 %all_to_all.15 = bf16[32,512,128]{2,1,0:T(8,128)(2,1)} all-to-all(bf16[32,512,128]{2,1,0:T(8,128)(2,1)S(1)} %stack.7), channel_id=1, replica_groups=mesh['row'=32,'col'=8,'vec'=2] {'row'}, dimensions={0} | all-to-all | bytes 8388608 | tf_op jit(solution)/shard_map/all_to_all | solution.py:31
  284.9 3.1 gather_fusion.1
  288.1 6.6 %fusion.8 = f32[32,128,256]{2,1,0:T(8,128)} fusion(bf16[1,1,32,256,256]{4,3,2,1,0:T(8,128)(2,1)} %param.8, bf16[32,256,128]{2,1,0:T(8,128)(2,1)S(1)} %gather_fusion.1, pred[32]{0:T(512)(128)(4,1)S(1)} %compare_and_fusion), kind=kOutput, calls=%fused_computation.11 | convolution fusion | flops 537919488 | bytes 10485792 | tf_op jit(solution)/shard_map/sij,sjk->sik/dot_general | solution.py:36
  294.6 5.5 %copy.10 = f32[32,128,256]{1,0,2:T(8,128)} copy(f32[32,128,256]{2,1,0:T(8,128)} %fusion.8) | data formatting | bytes 8388608 | tf_op jit(solution)/shard_map/sij,sjk->sik/dot_general | solution.py:36
  300.1 4.3 fusion.21
  304.4 1.2 copy.7
  305.6 0.0 reduce-scatter.6.cloned.1.call-update
  305.7 0.2 reduce-scatter.8.cloned.1.call-start
  305.9 39.3 %reduce-scatter.6.cloned.1.call-done = bf16[512,128]{1,0:T(8,128)(2,1)} async-done(((bf16[4096,128]{1,0:T(8,128)(2,1)}), bf16[512,128]{1,0:T(8,128)(2,1)}) %reduce-scatter.6.cloned.1.call-update) | async-done | bytes 131088 | tf_op jit(solution)/shard_map/reduce_scatter | solution.py:41
  345.2 1.0 fusion.33
  346.2 0.9 stack.8
  347.1 101.8 %all_to_all.16 = bf16[32,512,128]{2,1,0:T(8,128)(2,1)} all-to-all(bf16[32,512,128]{2,1,0:T(8,128)(2,1)S(1)} %stack.8), channel_id=1, replica_groups=mesh['row'=32,'col'=8,'vec'=2] {'row'}, dimensions={0} | all-to-all | bytes 8388608 | tf_op jit(solution)/shard_map/all_to_all | solution.py:31
  448.9 3.1 gather_fusion.2
  452.0 6.6 %fusion.6 = f32[32,128,256]{2,1,0:T(8,128)} fusion(bf16[1,1,32,256,256]{4,3,2,1,0:T(8,128)(2,1)} %param.8, bf16[32,256,128]{2,1,0:T(8,128)(2,1)S(1)} %gather_fusion.2, pred[32]{0:T(512)(128)(4,1)S(1)} %compare_and_fusion), kind=kOutput, calls=%fused_computation.9 | convolution fusion | flops 537919488 | bytes 10485792 | tf_op jit(solution)/shard_map/sij,sjk->sik/dot_general | solution.py:36
  458.6 5.5 %copy.11 = f32[32,128,256]{1,0,2:T(8,128)} copy(f32[32,128,256]{2,1,0:T(8,128)} %fusion.6) | data formatting | bytes 8388608 | tf_op jit(solution)/shard_map/sij,sjk->sik/dot_general | solution.py:36
  464.1 4.3 fusion.24
  468.4 1.2 copy.8
  469.6 0.0 reduce-scatter.8.cloned.1.call-update
  469.6 39.7 %reduce-scatter.8.cloned.1.call-done = bf16[512,128]{1,0:T(8,128)(2,1)} async-done(((bf16[4096,128]{1,0:T(8,128)(2,1)}), bf16[512,128]{1,0:T(8,128)(2,1)}) %reduce-scatter.8.cloned.1.call-update) | async-done | bytes 131088 | tf_op jit(solution)/shard_map/reduce_scatter | solution.py:41
  509.3 1.6 fusion.35
  (4 shorter events, 0.0 us)
Async XLA Ops:
  10.4 11.2 %copy-start.2 = (s32[1,1,32]{2,1,0:T(1,128)S(1)}, s32[1,1,32]{2,1,0:T(1,128)}, u32[]{:S(2)}) copy-start(s32[1,1,32]{2,1,0:T(1,128)} %param.10) | copy-start | bytes 388
  10.4 105.1 %all-to-all-start = ((bf16[32,512,128]{2,1,0:T(8,128)(2,1)}), bf16[32,512,128]{2,1,0:T(8,128)(2,1)}, u32[]{:S(2)}, u32[]{:S(2)}) async-start(bf16[32,512,128]{2,1,0:T(8,128)(2,1)} %stack.6), calls=%async_computation | async-start | bytes 8388608 | tf_op jit(solution)/shard_map/all_to_all | solution.py:31
  20.9 160.4 %reduce-scatter.4.cloned.1.call-start = ((), (), s32[]{:S(2)}) async-start(), calls=%async_computation.6 | async-start | bytes 1179648 | tf_op jit(solution)/shard_map/reduce_scatter | solution.py:41
  125.2 5.5 %copy-start.1 = (s32[1,1,32]{2,1,0:T(1,128)S(1)}, s32[1,1,32]{2,1,0:T(1,128)}, u32[]{:S(2)}) copy-start(s32[1,1,32]{2,1,0:T(1,128)} %param.9) | copy-start | bytes 388
  130.7 50.6 %copy-start = (bf16[512,128]{1,0:T(8,128)(2,1)S(1)}, bf16[512,128]{1,0:T(8,128)(2,1)}, u32[]{:S(2)}) copy-start(bf16[512,128]{1,0:T(8,128)(2,1)} %param.7) | copy-start | bytes 393220
  136.3 208.9 %reduce-scatter.6.cloned.1.call-start = ((), (), s32[]{:S(2)}) async-start(), calls=%async_computation.7 | async-start | bytes 1179648 | tf_op jit(solution)/shard_map/reduce_scatter | solution.py:41
  305.7 203.7 %reduce-scatter.8.cloned.1.call-start = ((), (), s32[]{:S(2)}) async-start(), calls=%async_computation.8 | async-start | bytes 1179648 | tf_op jit(solution)/shard_map/reduce_scatter | solution.py:41
Sparse Core Ops, SparseCore 0:
  136.4 44.8 reduce-scatter.3
  305.8 39.3 reduce-scatter.5
  469.8 39.4 reduce-scatter.7
